TPU v7x, 32 devices: a whole 2x2x4 slice. The times are simulated.
32 devices in a mesh: rcv: 4 (over y, core), slab: 8 (over z, x).
Axes of the slice: x: 2, y: 2, z: 4, core: 2. Of those that a mesh axis runs over, the one named last changes fastest.
Arguments:
- displacement: bfloat16 [2, 16, 3, 16, 16, 1024], P(None, None, None, 'slab'), may hold values from -6 to 6
- green: bfloat16 [8, 16, 6, 16, 16, 1024], P('rcv', None, None, 'slab'), may hold values from -0.1796875 to 0.1796875
- lame_lambda: float32 [16, 16, 1024], P('slab'), may hold values from 0.5 to 2
- shear_modulus: float32 [16, 16, 1024], P('slab'), may hold values from 0.3 to 1.5
- filters: float32 [2, 8, 9], P(None, 'rcv'), may hold values from -2 to 2
- pairs: int32 [2, 8], P(None, 'rcv'), may hold values 0 or 1
Outputs:
- kernels: float32 [2, 16, 16, 1024], P(None, 'slab', 'rcv')
Inputs may be any that keep to these rules, and one draw needn't show every extreme that they name: `pairs`: 1 marks a pair that is used, 0 one that is not.
All inputs are finite; a program needn't handle non-finite values. No bound on the sum of `pairs` on one device may be relied on, other than what follows from the above.
Results may differ from a plain program's by a relative error of at most 0.0029.
Values may be sent and summed in bfloat16 or wider, within the bound.
No kernel may reach another device: no remote copies, remote signals or barrier semaphores. Data moves between devices by JAX's collectives and lax.ppermute only.
A program may use at most 192 MiB of HBM per device.

v0:
```python
import jax
import jax.numpy as jnp
from jax import lax
from jax.sharding import PartitionSpec as P


def padded_2(array, sides, width):
    for axis, dim in sides:
        devices, length = (lax.axis_size(axis), array.shape[dim])
        up = [(i, (i + 1) % devices) for i in range(devices - 1)]
        down = [(j, i) for i, j in up]
        last = lax.slice_in_dim(array, length - width, length, axis=dim)
        initial = lax.slice_in_dim(array, 0, width, axis=dim)
        before = lax.ppermute(last, axis, up)
        after = lax.ppermute(initial, axis, down)
        array = jnp.concatenate([before, array, after], axis=dim)
    return array


def derivative(field, axis):
    length = field.shape[axis]
    pad_width = [(0, 0)] * field.ndim
    pad_width[axis] = (2, 2)
    padded = jnp.pad(field, pad_width)

    def window(offset):
        return lax.slice_in_dim(padded, 2 + offset, 2 + offset + length, axis=axis)

    return (8.0 * (window(1) - window(-1)) - (window(2) - window(-2))) / 12.0


def depth_derivative(extended, length):

    def window(offset):
        return lax.slice_in_dim(extended, 2 + offset, 2 + offset + length, axis=3)

    return (8.0 * (window(1) - window(-1)) - (window(2) - window(-2))) / 12.0


def compose(along_cols, along_rows, along_depth, lame_lambda, shear_modulus):
    strain_xx = along_cols[:, :, 0]
    strain_yy = along_rows[:, :, 1]
    strain_zz = along_depth[:, :, 2]
    strain_yz = 0.5 * (along_depth[:, :, 1] + along_rows[:, :, 2])
    strain_xz = 0.5 * (along_depth[:, :, 0] + along_cols[:, :, 2])
    strain_xy = 0.5 * (along_rows[:, :, 0] + along_cols[:, :, 1])
    strain_trace = strain_xx + strain_yy + strain_zz
    volume_term = lame_lambda * strain_trace
    double_shear = 2.0 * shear_modulus
    components = [
        volume_term + double_shear * strain_xx,
        volume_term + double_shear * strain_yy,
        volume_term + double_shear * strain_zz,
        double_shear * strain_yz,
        double_shear * strain_xz,
        double_shear * strain_xy,
    ]
    return jnp.stack(components, axis=2).astype(jnp.bfloat16)


def contribution(stress_one, filter_taps, green_one):
    lag_total = filter_taps.shape[0]
    half_lags = lag_total // 2
    snap_count = stress_one.shape[0]
    padded = jnp.pad(stress_one, [(half_lags, half_lags)] + [(0, 0)] * (stress_one.ndim - 1))
    filtered = jnp.zeros(stress_one.shape, jnp.float32)
    for lag_index in range(lag_total):
        filtered = filtered + filter_taps[lag_index] * padded[
            lag_index : lag_index + snap_count
        ].astype(jnp.float32)
    weights = jnp.array([1.0, 1.0, 1.0, 2.0, 2.0, 2.0], jnp.float32).reshape(1, 6, 1, 1, 1)
    return jnp.sum(filtered * green_one.astype(jnp.float32) * weights, axis=(0, 1))


def on_device(displacement, green, lame_lambda, shear_modulus, filters, pairs):
    sources, snap_count, components, planes, row_count, col_count = displacement.shape
    groups = lax.axis_size("rcv")
    member = lax.axis_index("rcv")
    flat = displacement.reshape((sources * snap_count, components, planes, row_count, col_count))
    share = flat.shape[0] // groups
    mine = lax.dynamic_slice_in_dim(flat, member * share, share, 0)
    grown = padded_2(mine, (("slab", 2),), 2)
    edges = jnp.concatenate([grown[:, :, 0:2], grown[:, :, planes + 2 : planes + 4]], axis=2)
    every_edge = lax.all_gather(edges, "rcv", axis=0, tiled=True)
    joined = jnp.concatenate([every_edge[:, :, 0:2], flat, every_edge[:, :, 2:4]], axis=2)
    extended = joined.reshape((sources, snap_count, components, planes + 4, row_count, col_count))
    field = extended.astype(jnp.float32)
    interior = field[:, :, :, 2 : planes + 2]
    along_depth = depth_derivative(field, planes)
    along_rows = derivative(interior, 4)
    along_cols = derivative(interior, 5)
    stress = compose(along_cols, along_rows, along_depth, lame_lambda, shear_modulus)
    station_count = green.shape[0]
    slots = sources * station_count
    flat_pairs = pairs.reshape(-1)
    initial = jnp.zeros((sources, planes, row_count, col_count), jnp.float32)

    def add_slot(slot, kernel_acc, weight):
        source = slot // station_count
        station = slot % station_count
        stress_one = lax.dynamic_index_in_dim(stress, source, 0, keepdims=False)
        green_one = lax.dynamic_index_in_dim(green, station, 0, keepdims=False)
        filter_taps = filters[source, station]
        term = weight * contribution(stress_one, filter_taps, green_one)
        current = lax.dynamic_index_in_dim(kernel_acc, source, 0, keepdims=False)
        return lax.dynamic_update_index_in_dim(kernel_acc, current + term, source, 0)

    def add_masked(slot, kernel_acc):
        return add_slot(slot, kernel_acc, flat_pairs[slot].astype(jnp.float32))

    kernel_acc = lax.fori_loop(0, slots, add_masked, initial)
    return lax.psum_scatter(kernel_acc, "rcv", scatter_dimension=2, tiled=True)


def solution(mesh):
    placed = (
        P(None, None, None, "slab", None, None),
        P("rcv", None, None, "slab", None, None),
        P("slab", None, None),
        P("slab", None, None),
        P(None, "rcv", None),
        P(None, "rcv"),
    )
    return jax.shard_map(
        on_device,
        mesh=mesh,
        in_specs=placed,
        out_specs=P(None, "slab", "rcv", None),
        check_vma=False,
    )
```

profile of v0, /device:TPU:0, one launch (start us, length us, event | category | flops | bytes accessed | tf_op | source)
XLA Modules:
  0.0 495.1 jit_solution(11546847999297486046)
XLA Ops:
  6.5 0.0 copy-start.5
  6.5 0.0 copy-start.2
  6.5 0.0 all-gather.2.cloned.1.call-start
  6.5 1.6 constant_dynamic-slice_fusion.2
  8.2 5.0 %collective-permute-start = (bf16[8,3,2,16,1024]{4,3,2,1,0:T(8,128)(2,1)S(1)}, bf16[8,3,2,16,1024]{4,3,2,1,0:T(8,128)(2,1)S(1)}, u32[]{:S(2)}, u32[]{:S(2)}) collective-permute-start(bf16[8,3,2,16,1024]{4,3,2,1,0:T(8,128)(2,1)S(1)} %constant_dynamic-slice_fusion.2), channel_id=1, source_target_pairs={{0,1},{1,2},{2,3},{3,4},{4,5},{5,6},{6,7},{8,9},{9,10},{10,11},{11... | collective-permute-start | bytes 4718600 | tf_op jit(solution)/shard_map/ppermute | solution.py:14
  13.1 1.3 collective-permute-start.1
  14.4 65.9 %collective-permute-done = bf16[8,3,2,16,1024]{4,3,2,1,0:T(8,128)(2,1)S(1)} collective-permute-done((bf16[8,3,2,16,1024]{4,3,2,1,0:T(8,128)(2,1)S(1)}, bf16[8,3,2,16,1024]{4,3,2,1,0:T(8,128)(2,1)S(1)}, u32[]{:S(2)}, u32[]{:S(2)}) %collective-permute-start) | collective-permute-done | bytes 1572896 | tf_op jit(solution)/shard_map/ppermute | solution.py:14
  80.4 0.0 collective-permute-done.1
  80.4 1.9 pad_maximum_fusion
  82.3 0.0 all-gather.2.cloned.1.call-update
  82.3 0.0 all-reduce.6.cloned.1.call-start
  82.4 0.0 copy-done.5
  82.4 0.1 reshape.52
  82.5 0.0 copy-done.2
  82.5 84.3 %all-gather.2.cloned.1.call-done = bf16[32,3,4,16,1024]{4,3,2,1,0:T(8,128)(2,1)} async-done(((bf16[8,3,4,16,1024]{4,3,2,1,0:T(8,128)(2,1)}), bf16[32,3,4,16,1024]{4,3,2,1,0:T(8,128)(2,1)}) %all-gather.2.cloned.1.call-update) | async-done | bytes 12582928 | tf_op jit(solution)/shard_map/all_gather | solution.py:84
  166.8 5.6 %fusion.29 = (bf16[32,3,2,16,1024]{4,3,2,1,0:T(8,128)(2,1)S(1)}, bf16[32,3,2,16,1024]{4,3,2,1,0:T(8,128)(2,1)S(1)}) fusion(bf16[32,3,4,16,1024]{4,3,2,1,0:T(8,128)(2,1)} %all-gather.2.cloned.1.call-done), kind=kLoop, calls=%fused_computation.63 | loop fusion | bytes 25165824 | tf_op jit(solution)/shard_map/slice | solution.py:85
  172.3 14.7 %maximum_convert_fusion = f32[2,16,3,6,16,1024]{5,4,3,2,1,0:T(8,128)} fusion(bf16[2,16,3,2,16,1024]{5,4,3,2,1,0:T(8,128)(2,1)S(1)} %bitcast.54, bf16[2,16,3,2,16,1024]{5,4,3,2,1,0:T(8,128)(2,1)} %param.9, bf16[2,16,3,2,16,1024]{5,4,3,2,1,0:T(8,128)(2,1)S(1)} %bitcast.53), kind=kLoop, calls=%fused_computation.19 | loop fusion | flops 28311552 | bytes 56623104 | tf_op jit(solution)/shard_map/convert_element_type | solution.py:87
  187.0 31.9 %fusion.14 = (f32[2,16,3,2,16,1024]{5,4,3,2,1,0:T(8,128)}, f32[2,16,3,2,16,1024]{5,4,3,2,1,0:T(8,128)}) fusion(f32[2,16,3,6,16,1024]{5,4,3,2,1,0:T(8,128)} %maximum_convert_fusion), kind=kLoop, calls=%fused_computation.36 | loop fusion | flops 15728640 | bytes 88080384 | tf_op jit(solution)/shard_map/div | solution.py:37
  218.9 43.1 %fusion.11 = (f32[2,16,3,2,16,1024]{5,4,3,2,1,0:T(8,128)}, f32[2,16,3,2,16,1024]{5,4,3,2,1,0:T(8,128)}) fusion(f32[2,16,3,2,16,1024]{5,4,3,2,1,0:T(8,128)} %get-tuple-element.231), kind=kLoop, calls=%fused_computation.32 | loop fusion | flops 31457280 | bytes 37748736 | tf_op jit(solution)/shard_map/div | solution.py:29
  262.0 0.0 copy-done.3
  262.0 6.4 %fusion.22 = (bf16[2,16,6,2,16,1024]{5,4,3,2,1,0:T(8,128)(2,1)S(1)}, f32[2,16,1,2,16,1024]{5,4,3,2,1,0:T(8,128)S(1)}) fusion(f32[2,16,3,2,16,1024]{5,4,3,2,1,0:T(8,128)} %get-tuple-element.233, f32[2,16,1024]{2,1,0:T(8,128)S(1)} %broadcast_multiply_fusion, f32[2,16,3,2,16,1024]{5,4,3,2,1,0:T(8,128)} %get-tuple-element.230, ...), kind=kLoop, calls=%fused_computation.53 | loop fusion | flops 6291455 | bytes 19136512
  268.4 0.0 slice-start
  268.4 3.5 fusion.23
  271.9 0.0 slice-start.1
  271.9 3.5 fusion.24
  275.3 0.0 slice-start.2
  275.4 4.7 fusion.25
  280.1 0.0 slice-done
  280.1 0.0 slice-done.1
  280.1 0.0 slice-done.2
  280.1 0.0 copy-start.4
  280.1 3.3 fusion.26
  283.5 3.3 fusion.27
  286.8 0.0 copy-start
  286.8 4.5 copy-done
  291.3 0.0 copy-done.4
  291.3 162.3 %while.16 = (s32[]{:T(128)}, f32[2,2,16,1024]{3,2,1,0:T(8,128)S(1)}, s32[4]{0:T(128)S(1)}, f32[2,2,9]{2,1,0:T(2,128)}, bf16[2,16,6,2,16,1024]{5,4,3,2,1,0:T(8,12...) while((s32[]{:T(128)}, ...), condition=%wide.region_2.3_spmd.clone, body=%wide.region_0.2_spmd.sunk.clone.sunk | while | flops 94404624 | bytes 25690652 | solution.py:111
  291.3 6.8 %dynamic-slice_bitcast_fusion.2 = bf16[16,6,2,16,1024]{4,3,2,1,0:T(8,128)(2,1)} fusion(bf16[2,16,6,2,16,1024]{5,4,3,2,1,0:T(8,128)(2,1)} %get-tuple-element.317, s32[]{:T(128)S(6)} %select_n.84), kind=kLoop, calls=%fused_computation.11.clone.1 | loop fusion | bytes 12582916 | tf_op jit(solution)/shard_map/while/body/eval_jaxpr/jit(dynamic_index_in_dim)/squeeze | solution.py:101
  298.1 0.7 constant_dynamic-slice_fusion.4
  298.8 0.7 fusion.33
  299.4 31.1 %fusion.34 = f32[2,16,1024]{2,1,0:T(8,128)S(1)} fusion(bf16[16,6,2,16,1024]{4,3,2,1,0:T(8,128)(2,1)} %dynamic-slice_bitcast_fusion.2, f32[6]{0:T(128)S(1)} %get-tuple-element.323, bf16[2,16,6,2,16,1024]{5,4,3,2,1,0:T(8,128)(2,1)} %get-tuple-element.318, s32[]{:T(128)S(6)} %select_n.86, f32[]{:T(128)} %bitcast.41, f32[]{:T(128)} %bitcast.42, ...), kind=kLoop, calls=%fused_computation.10.clone.1 | loop fusion | flops 94339072 | bytes 12714048 | tf_op jit(solution)/shard_map/while/body/eval_jaxpr/reduce_sum | solution.py:72
  330.6 0.6 dynamic_slice.80
  331.8 6.8 %dynamic-slice_bitcast_fusion.2 = bf16[16,6,2,16,1024]{4,3,2,1,0:T(8,128)(2,1)} fusion(bf16[2,16,6,2,16,1024]{5,4,3,2,1,0:T(8,128)(2,1)} %get-tuple-element.317, s32[]{:T(128)S(6)} %select_n.84), kind=kLoop, calls=%fused_computation.11.clone.1 | loop fusion | bytes 12582916 | tf_op jit(solution)/shard_map/while/body/eval_jaxpr/jit(dynamic_index_in_dim)/squeeze | solution.py:101
  338.6 0.7 constant_dynamic-slice_fusion.4
  339.3 0.7 fusion.33
  340.0 31.2 %fusion.34 = f32[2,16,1024]{2,1,0:T(8,128)S(1)} fusion(bf16[16,6,2,16,1024]{4,3,2,1,0:T(8,128)(2,1)} %dynamic-slice_bitcast_fusion.2, f32[6]{0:T(128)S(1)} %get-tuple-element.323, bf16[2,16,6,2,16,1024]{5,4,3,2,1,0:T(8,128)(2,1)} %get-tuple-element.318, s32[]{:T(128)S(6)} %select_n.86, f32[]{:T(128)} %bitcast.41, f32[]{:T(128)} %bitcast.42, ...), kind=kLoop, calls=%fused_computation.10.clone.1 | loop fusion | flops 94339072 | bytes 12714048 | tf_op jit(solution)/shard_map/while/body/eval_jaxpr/reduce_sum | solution.py:72
  371.2 0.6 dynamic_slice.80
  372.5 6.8 %dynamic-slice_bitcast_fusion.2 = bf16[16,6,2,16,1024]{4,3,2,1,0:T(8,128)(2,1)} fusion(bf16[2,16,6,2,16,1024]{5,4,3,2,1,0:T(8,128)(2,1)} %get-tuple-element.317, s32[]{:T(128)S(6)} %select_n.84), kind=kLoop, calls=%fused_computation.11.clone.1 | loop fusion | bytes 12582916 | tf_op jit(solution)/shard_map/while/body/eval_jaxpr/jit(dynamic_index_in_dim)/squeeze | solution.py:101
  379.2 0.7 constant_dynamic-slice_fusion.4
  379.9 0.7 fusion.33
  380.6 31.1 %fusion.34 = f32[2,16,1024]{2,1,0:T(8,128)S(1)} fusion(bf16[16,6,2,16,1024]{4,3,2,1,0:T(8,128)(2,1)} %dynamic-slice_bitcast_fusion.2, f32[6]{0:T(128)S(1)} %get-tuple-element.323, bf16[2,16,6,2,16,1024]{5,4,3,2,1,0:T(8,128)(2,1)} %get-tuple-element.318, s32[]{:T(128)S(6)} %select_n.86, f32[]{:T(128)} %bitcast.41, f32[]{:T(128)} %bitcast.42, ...), kind=kLoop, calls=%fused_computation.10.clone.1 | loop fusion | flops 94339072 | bytes 12714048 | tf_op jit(solution)/shard_map/while/body/eval_jaxpr/reduce_sum | solution.py:72
  411.7 0.6 dynamic_slice.80
  413.0 6.8 %dynamic-slice_bitcast_fusion.2 = bf16[16,6,2,16,1024]{4,3,2,1,0:T(8,128)(2,1)} fusion(bf16[2,16,6,2,16,1024]{5,4,3,2,1,0:T(8,128)(2,1)} %get-tuple-element.317, s32[]{:T(128)S(6)} %select_n.84), kind=kLoop, calls=%fused_computation.11.clone.1 | loop fusion | bytes 12582916 | tf_op jit(solution)/shard_map/while/body/eval_jaxpr/jit(dynamic_index_in_dim)/squeeze | solution.py:101
  419.8 0.7 constant_dynamic-slice_fusion.4
  420.4 0.7 fusion.33
  421.1 31.2 %fusion.34 = f32[2,16,1024]{2,1,0:T(8,128)S(1)} fusion(bf16[16,6,2,16,1024]{4,3,2,1,0:T(8,128)(2,1)} %dynamic-slice_bitcast_fusion.2, f32[6]{0:T(128)S(1)} %get-tuple-element.323, bf16[2,16,6,2,16,1024]{5,4,3,2,1,0:T(8,128)(2,1)} %get-tuple-element.318, s32[]{:T(128)S(6)} %select_n.86, f32[]{:T(128)} %bitcast.41, f32[]{:T(128)} %bitcast.42, ...), kind=kLoop, calls=%fused_computation.10.clone.1 | loop fusion | flops 94339072 | bytes 12714048 | tf_op jit(solution)/shard_map/while/body/eval_jaxpr/reduce_sum | solution.py:72
  452.3 0.6 dynamic_slice.80
  453.6 0.0 copy-start.1
  453.6 0.7 copy-done.1
  454.3 0.0 all-reduce.6.cloned.1.call-update
  454.3 0.0 copy-done.6
  454.3 0.6 dynamic-slice
  455.5 31.2 %all-reduce.6.cloned.1.call-done = f32[2,2,16,1024]{3,2,1,0:T(8,128)} async-done(((f32[2,2,16,1024]{3,2,1,0:T(8,128)}), f32[2,2,16,1024]{3,2,1,0:T(8,128)}) %all-reduce.6.cloned.1.call-update) | async-done | bytes 262160
  486.7 1.5 constant_dynamic-slice_fusion.1
  (9 shorter events, 0.1 us)
Async XLA Ops:
  6.5 75.8 %copy-start.5 = (s32[2,2]{1,0:T(2,128)S(1)}, s32[2,2]{1,0:T(2,128)}, u32[]{:S(2)}) copy-start(s32[2,2]{1,0:T(2,128)} %param.14) | copy-start | bytes 52
  6.5 75.9 %copy-start.2 = (f32[2,16,1024]{2,1,0:T(8,128)S(1)}, f32[2,16,1024]{2,1,0:T(8,128)}, u32[]{:S(2)}) copy-start(f32[2,16,1024]{2,1,0:T(8,128)} %param.12) | copy-start | bytes 393220
  6.5 160.2 %all-gather.2.cloned.1.call-start = ((), (), s32[]{:S(2)}) async-start(), calls=%async_computation | async-start | bytes 15728640 | tf_op jit(solution)/shard_map/all_gather | solution.py:84
  8.2 72.2 %collective-permute-start = (bf16[8,3,2,16,1024]{4,3,2,1,0:T(8,128)(2,1)S(1)}, bf16[8,3,2,16,1024]{4,3,2,1,0:T(8,128)(2,1)S(1)}, u32[]{:S(2)}, u32[]{:S(2)}) collective-permute-start(bf16[8,3,2,16,1024]{4,3,2,1,0:T(8,128)(2,1)S(1)} %constant_dynamic-slice_fusion.2), channel_id=1, source_target_pairs={{0,1},{1,2},{2,3},{3,4},{4,5},{5,6},{6,7},{8,9},{9,10},{10,11},{11... | collective-permute-start | bytes 4718600 | tf_op jit(solution)/shard_map/ppermute | solution.py:14
  13.1 67.2 %collective-permute-start.1 = (bf16[8,3,2,16,1024]{4,3,2,1,0:T(8,128)(2,1)S(1)}, bf16[8,3,2,16,1024]{4,3,2,1,0:T(8,128)(2,1)S(1)}, u32[]{:S(2)}, u32[]{:S(2)}) collective-permute-start(bf16[8,3,2,16,1024]{4,3,2,1,0:T(8,128)(2,1)S(1)} %constant_dynamic-slice_fusion.2), channel_id=1, source_target_pairs={{1,0},{2,1},{3,2},{4,3},{5,4},{6,5},{7,6},{9,8},{10,9},{11,10},{12... | collective-permute-start | bytes 4718600 | tf_op jit(solution)/shard_map/ppermute | solution.py:15
  82.3 404.4 %all-reduce.6.cloned.1.call-start = ((), (), s32[]{:S(2)}) async-start(), calls=%async_computation.1 | async-start | bytes 524288
  218.9 43.1 %copy-start.3 = (f32[2,16,1024]{2,1,0:T(8,128)S(1)}, f32[2,16,1024]{2,1,0:T(8,128)}, u32[]{:S(2)}) copy-start(f32[2,16,1024]{2,1,0:T(8,128)} %param.11) | copy-start | bytes 393220
  268.4 11.7 %slice-start = ((s8[12582912]{0:T(1024)(128)(4,1)}), s8[4194304]{0:T(1024)(128)(4,1)S(1)}, s32[]{:S(2)}) async-start(s8[12582912]{0:T(1024)(128)(4,1)} %bitcast.51), calls=%async_computation.2 | async-start | bytes 8388608
  271.9 8.2 %slice-start.1 = ((s8[12582912]{0:T(1024)(128)(4,1)}), s8[4194304]{0:T(1024)(128)(4,1)S(1)}, s32[]{:S(2)}) async-start(s8[12582912]{0:T(1024)(128)(4,1)} %bitcast.51), calls=%async_computation.3 | async-start | bytes 8388608
  275.3 4.8 slice-start.2
  280.1 11.2 %copy-start.4 = (f32[6]{0:T(128)S(1)}, f32[6]{0:T(128)}, u32[]{:S(2)}) copy-start(f32[6]{0:T(128)} %constant.131.clone..sunk.2) | copy-start | bytes 76
  286.8 4.5 copy-start
  291.3 163.0 %copy-start.6 = (u32[32]{0:T(128)S(1)}, u32[32]{0:T(128)}, u32[]{:S(2)}) copy-start(u32[32]{0:T(128)} %constant.146) | copy-start | bytes 388
  453.6 0.7 copy-start.1
Sparse Core Ops, SparseCore 0:
  82.4 84.2 all-gather.1
  454.4 32.2 all-reduce.5
where the time goes:
time: 496 us; the launch traced here: 495 us
  other arithmetic  241 us (49%)
  waiting for transfers between devices  181 us (36%)
  local copies, waits for them, and re-layouts  49.5 us (10%)
  between operations  14.2 us (3%)
  starting transfers between devices  6.31 us (1%)
    reduce_sum x4, other arithmetic, contribution(): jnp.sum(filtered * green_one.astype(jnp.float32) * weights, axis=(0, 1))  125 us
    all_gather x1, waiting for transfers between devices, on_device(): every_edge = lax.all_gather(edges, 'rcv', axis=0, tiled=True)  84.3 us
    ppermute x1, waiting for transfers between devices, padded_2(): before = lax.ppermute(last, axis, up)  65.9 us
    div x1, other arithmetic, derivative(): return (8.0 * (window(1) - window(-1)) - (window(2) - window(-2))) / 12.0  43.1 us
    div x1, other arithmetic, depth_derivative(): return (8.0 * (window(1) - window(-1)) - (window(2) - window(-2))) / 12.0  31.9 us
    unnamed x3, waiting for transfers between devices  31.2 us
    squeeze x4, local copies, waits for them, and re-layouts, add_slot(): stress_one = lax.dynamic_index_in_dim(stress, source, 0, keepdims=False)  27.1 us
    unnamed x6, other arithmetic  21.3 us
  transfers between devices with their start and end apart: 4, of which 3 were waited for; matrix products, arithmetic and copies ran while one was open for 0% of the time, Pallas kernels for 0%

commit v1 on v0

--- a/solution.py
+++ b/solution.py
@@ -81,7 +81,12 @@
     mine = lax.dynamic_slice_in_dim(flat, member * share, share, 0)
     grown = padded_2(mine, (("slab", 2),), 2)
     edges = jnp.concatenate([grown[:, :, 0:2], grown[:, :, planes + 2 : planes + 4]], axis=2)
-    every_edge = lax.all_gather(edges, "rcv", axis=0, tiled=True)
+    ring = [edges]
+    for hop in range(3):
+        ring.append(lax.ppermute(ring[-1], "rcv", [(dev, (dev + 1) % 4) for dev in range(4)]))
+    every_edge = jnp.roll(
+        jnp.concatenate(ring[::-1], axis=0), (lax.axis_index("rcv") + 1) * ring[0].shape[0], axis=0
+    )
     joined = jnp.concatenate([every_edge[:, :, 0:2], flat, every_edge[:, :, 2:4]], axis=2)
     extended = joined.reshape((sources, snap_count, components, planes + 4, row_count, col_count))
     field = extended.astype(jnp.float32)

time: 496 us -> 563 us (1.14)
  local copies, waits for them, and re-layouts: 49.5 us -> 84.7 us
  waiting for transfers between devices: 181 us -> 208 us
    ppermute x0 -> x3, waiting for transfers between devices: none -> 109 us  [on_device(): lax.ppermute(ring[-1], 'rcv', [(dev, (dev + 1) % 4) for dev in range(4)])]
    all_gather x1 -> x0, waiting for transfers between devices: 84.3 us -> none  [on_device(): every_edge = lax.all_gather(edges, 'rcv', axis=0, tiled=True)]
    unnamed x22 -> x33, local copies, waits for them, and re-layouts: 7.35 us -> 33.9 us
    slice x1, local copies, waits for them, and re-layouts: 5.56 us -> 12.1 us  [on_device(): every_edge[:, :, 0:2]]
    unnamed x3 -> x2, waiting for transfers between devices: 31.2 us -> 33.4 us
  transfers between devices with their start and end apart: 4 -> 6, of which waited for: 3 -> 5; matrix products, arithmetic and copies ran while one was open for 0% -> 0% of each run, Pallas kernels for 0% -> 0%
where the time goes in v1:
time: 563 us; the launch traced here: 562 us
  other arithmetic  246 us (44%)
  waiting for transfers between devices  208 us (37%)
  local copies, waits for them, and re-layouts  84.7 us (15%)
  between operations  14.2 us (3%)
  starting transfers between devices  6.33 us (1%)
    reduce_sum x4, other arithmetic, contribution(): jnp.sum(filtered * green_one.astype(jnp.float32) * weights, axis=(0, 1))  124 us
    ppermute x3, waiting for transfers between devices, on_device(): lax.ppermute(ring[-1], 'rcv', [(dev, (dev + 1) % 4) for dev in range(4)])  109 us
    ppermute x1, waiting for transfers between devices, padded_2(): before = lax.ppermute(last, axis, up)  65.9 us
    div x1, other arithmetic, derivative(): return (8.0 * (window(1) - window(-1)) - (window(2) - window(-2))) / 12.0  43.4 us
    unnamed x33, local copies, waits for them, and re-layouts  33.9 us
    unnamed x2, waiting for transfers between devices  33.4 us
    div x1, other arithmetic, depth_derivative(): return (8.0 * (window(1) - window(-1)) - (window(2) - window(-2))) / 12.0  31.9 us
    squeeze x4, local copies, waits for them, and re-layouts, add_slot(): stress_one = lax.dynamic_index_in_dim(stress, source, 0, keepdims=False)  27.1 us
  transfers between devices with their start and end apart: 6, of which 5 were waited for; matrix products, arithmetic and copies ran while one was open for 0% of the time, Pallas kernels for 0%

profile of v1, /device:TPU:0, one launch (start us, length us, event | category | flops | bytes accessed | tf_op | source)
XLA Modules:
  0.0 561.8 jit_solution(17714681269376043942)
XLA Ops:
  6.5 1.6 constant_dynamic-slice_fusion.3
  8.1 5.0 collective-permute-start
  13.1 1.3 collective-permute-start.1
  14.4 65.9 %collective-permute-done = bf16[8,3,2,16,1024]{4,3,2,1,0:T(8,128)(2,1)S(1)} collective-permute-done((bf16[8,3,2,16,1024]{4,3,2,1,0:T(8,128)(2,1)S(1)}, bf16[8,3,2,16,1024]{4,3,2,1,0:T(8,128)(2,1)S(1)}, u32[]{:S(2)}, u32[]{:S(2)}) %collective-permute-start) | collective-permute-done | bytes 1572896 | tf_op jit(solution)/shard_map/ppermute | solution.py:14
  80.3 0.0 collective-permute-done.1
  80.3 0.3 pad_maximum_fusion
  80.6 0.1 collective-permute-start.2
  80.7 36.7 %collective-permute-done.2 = bf16[8,3,4,16,1024]{4,3,2,1,0:T(8,128)(2,1)S(1)} collective-permute-done((bf16[8,3,4,16,1024]{4,3,2,1,0:T(8,128)(2,1)S(1)}, bf16[8,3,4,16,1024]{4,3,2,1,0:T(8,128)(2,1)S(1)}, u32[]{:S(2)}, u32[]{:S(2)}) %collective-permute-start.2) | collective-permute-done | bytes 3145760 | tf_op jit(solution)/shard_map/ppermute | solution.py:86
  117.4 1.6 copy-done.1
  119.0 0.0 collective-permute-start.3
  119.0 36.8 %collective-permute-done.3 = bf16[8,3,4,16,1024]{4,3,2,1,0:T(8,128)(2,1)} collective-permute-done((bf16[8,3,4,16,1024]{4,3,2,1,0:T(8,128)(2,1)S(1)}, bf16[8,3,4,16,1024]{4,3,2,1,0:T(8,128)(2,1)}, u32[]{:S(2)}, u32[]{:S(2)}) %collective-permute-start.3) | collective-permute-done | bytes 3145760 | tf_op jit(solution)/shard_map/ppermute | solution.py:86
  155.8 0.8 reshape.52
  156.6 1.1 broadcast_multiply_fusion
  157.6 35.2 %collective-permute-done.4 = bf16[8,3,4,16,1024]{4,3,2,1,0:T(8,128)(2,1)} collective-permute-done((bf16[8,3,4,16,1024]{4,3,2,1,0:T(8,128)(2,1)}, bf16[8,3,4,16,1024]{4,3,2,1,0:T(8,128)(2,1)}, u32[]{:S(2)}, u32[]{:S(2)}) %collective-permute-start.4) | collective-permute-done | bytes 3145760 | tf_op jit(solution)/shard_map/ppermute | solution.py:86
  192.8 4.1 constant_dynamic-update-slice_fusion.9
  196.9 4.1 constant_dynamic-update-slice_fusion.8
  201.1 2.3 constant_dynamic-update-slice_fusion.7
  203.3 1.4 constant_dynamic-update-slice_fusion.6
  204.7 1.3 constant_dynamic-update-slice_fusion.5
  206.0 4.1 constant_dynamic-update-slice_fusion.4
  210.1 4.1 constant_dynamic-update-slice_fusion.3
  214.2 2.3 constant_dynamic-update-slice_fusion.2
  216.5 1.3 constant_dynamic-update-slice_fusion.1
  217.8 1.3 constant_dynamic-update-slice_fusion
  219.1 12.1 %constant_dynamic-slice_fusion.1 = (bf16[32,3,2,16,1024]{4,3,2,1,0:T(8,128)(2,1)}, bf16[32,3,2,16,1024]{4,3,2,1,0:T(8,128)(2,1)}) fusion(bf16[64,3,4,16,1024]{4,3,2,1,0:T(8,128)(2,1)} %constant_dynamic-update-slice_fusion, s32[]{:T(128)S(6)} %select_n.85, s32[]{:T(128)S(6)} %add.263), kind=kLoop, calls=%fused_computation.70 | loop fusion | bytes 25165832 | tf_op jit(solution)/shard_map/slice | solution.py:90
  231.2 20.2 %maximum_convert_fusion = f32[2,16,3,6,16,1024]{5,4,3,2,1,0:T(8,128)} fusion(bf16[2,16,3,2,16,1024]{5,4,3,2,1,0:T(8,128)(2,1)} %bitcast.54, bf16[2,16,3,2,16,1024]{5,4,3,2,1,0:T(8,128)(2,1)} %param.9, bf16[2,16,3,2,16,1024]{5,4,3,2,1,0:T(8,128)(2,1)} %bitcast.53), kind=kLoop, calls=%fused_computation.19 | loop fusion | flops 28311552 | bytes 56623104 | tf_op jit(solution)/shard_map/convert_element_type | solution.py:92
  251.5 31.9 %fusion.14 = (f32[2,16,3,2,16,1024]{5,4,3,2,1,0:T(8,128)}, f32[2,16,3,2,16,1024]{5,4,3,2,1,0:T(8,128)}) fusion(f32[2,16,3,6,16,1024]{5,4,3,2,1,0:T(8,128)} %maximum_convert_fusion), kind=kLoop, calls=%fused_computation.36 | loop fusion | flops 15728640 | bytes 88080384 | tf_op jit(solution)/shard_map/div | solution.py:37
  283.4 43.4 %fusion.11 = (f32[2,16,3,2,16,1024]{5,4,3,2,1,0:T(8,128)}, f32[2,16,3,2,16,1024]{5,4,3,2,1,0:T(8,128)}) fusion(f32[2,16,3,2,16,1024]{5,4,3,2,1,0:T(8,128)} %get-tuple-element.231), kind=kLoop, calls=%fused_computation.32 | loop fusion | flops 31457280 | bytes 37748736 | tf_op jit(solution)/shard_map/div | solution.py:29
  326.8 6.3 %fusion.22 = (bf16[2,16,6,2,16,1024]{5,4,3,2,1,0:T(8,128)(2,1)S(1)}, f32[2,16,1,2,16,1024]{5,4,3,2,1,0:T(8,128)S(1)}) fusion(f32[2,16,3,2,16,1024]{5,4,3,2,1,0:T(8,128)} %get-tuple-element.235, f32[2,16,1024]{2,1,0:T(8,128)S(1)} %broadcast_multiply_fusion, f32[2,16,3,2,16,1024]{5,4,3,2,1,0:T(8,128)} %get-tuple-element.230, ...), kind=kLoop, calls=%fused_computation.53 | loop fusion | flops 6291455 | bytes 19136512
  333.2 0.0 copy-start.4
  333.2 0.0 slice-start
  333.2 3.5 fusion.23
  336.7 3.5 fusion.24
  340.2 4.7 fusion.25
  344.9 0.0 copy-start.6
  345.0 3.3 fusion.26
  348.3 3.3 fusion.27
  351.6 4.5 copy-done
  356.1 161.9 %while.16 = (s32[]{:T(128)}, f32[2,2,16,1024]{3,2,1,0:T(8,128)S(1)}, s32[4]{0:T(128)S(1)}, f32[2,2,9]{2,1,0:T(2,128)}, bf16[2,16,6,2,16,1024]{5,4,3,2,1,0:T(8,12...) while((s32[]{:T(128)}, ...), condition=%wide.region_2.3_spmd.clone, body=%wide.region_0.2_spmd.sunk.clone.sunk | while | flops 94404624 | bytes 25690652 | solution.py:116
  356.1 6.8 %dynamic-slice_bitcast_fusion.2 = bf16[16,6,2,16,1024]{4,3,2,1,0:T(8,128)(2,1)} fusion(bf16[2,16,6,2,16,1024]{5,4,3,2,1,0:T(8,128)(2,1)} %get-tuple-element.317, s32[]{:T(128)S(6)} %select_n.99), kind=kLoop, calls=%fused_computation.11.clone.1 | loop fusion | bytes 12582916 | tf_op jit(solution)/shard_map/while/body/eval_jaxpr/jit(dynamic_index_in_dim)/squeeze | solution.py:106
  362.9 0.7 constant_dynamic-slice_fusion.6
  363.6 0.7 fusion.32
  364.2 31.1 %fusion.33 = f32[2,16,1024]{2,1,0:T(8,128)S(1)} fusion(bf16[16,6,2,16,1024]{4,3,2,1,0:T(8,128)(2,1)} %dynamic-slice_bitcast_fusion.2, f32[6]{0:T(128)S(1)} %get-tuple-element.323, bf16[2,16,6,2,16,1024]{5,4,3,2,1,0:T(8,128)(2,1)} %get-tuple-element.318, s32[]{:T(128)S(6)} %select_n.101, f32[]{:T(128)} %bitcast.41, f32[]{:T(128)} %bitcast.42, ...), kind=kLoop, calls=%fused_computation.10.clone.1 | loop fusion | flops 94339072 | bytes 12714048 | tf_op jit(solution)/shard_map/while/body/eval_jaxpr/reduce_sum | solution.py:72
  395.3 0.6 dynamic_slice.85
  396.6 6.8 %dynamic-slice_bitcast_fusion.2 = bf16[16,6,2,16,1024]{4,3,2,1,0:T(8,128)(2,1)} fusion(bf16[2,16,6,2,16,1024]{5,4,3,2,1,0:T(8,128)(2,1)} %get-tuple-element.317, s32[]{:T(128)S(6)} %select_n.99), kind=kLoop, calls=%fused_computation.11.clone.1 | loop fusion | bytes 12582916 | tf_op jit(solution)/shard_map/while/body/eval_jaxpr/jit(dynamic_index_in_dim)/squeeze | solution.py:106
  403.4 0.7 constant_dynamic-slice_fusion.6
  404.1 0.7 fusion.32
  404.7 31.1 %fusion.33 = f32[2,16,1024]{2,1,0:T(8,128)S(1)} fusion(bf16[16,6,2,16,1024]{4,3,2,1,0:T(8,128)(2,1)} %dynamic-slice_bitcast_fusion.2, f32[6]{0:T(128)S(1)} %get-tuple-element.323, bf16[2,16,6,2,16,1024]{5,4,3,2,1,0:T(8,128)(2,1)} %get-tuple-element.318, s32[]{:T(128)S(6)} %select_n.101, f32[]{:T(128)} %bitcast.41, f32[]{:T(128)} %bitcast.42, ...), kind=kLoop, calls=%fused_computation.10.clone.1 | loop fusion | flops 94339072 | bytes 12714048 | tf_op jit(solution)/shard_map/while/body/eval_jaxpr/reduce_sum | solution.py:72
  435.8 0.6 dynamic_slice.85
  437.1 6.8 %dynamic-slice_bitcast_fusion.2 = bf16[16,6,2,16,1024]{4,3,2,1,0:T(8,128)(2,1)} fusion(bf16[2,16,6,2,16,1024]{5,4,3,2,1,0:T(8,128)(2,1)} %get-tuple-element.317, s32[]{:T(128)S(6)} %select_n.99), kind=kLoop, calls=%fused_computation.11.clone.1 | loop fusion | bytes 12582916 | tf_op jit(solution)/shard_map/while/body/eval_jaxpr/jit(dynamic_index_in_dim)/squeeze | solution.py:106
  443.9 0.7 constant_dynamic-slice_fusion.6
  444.5 0.7 fusion.32
  445.2 31.1 %fusion.33 = f32[2,16,1024]{2,1,0:T(8,128)S(1)} fusion(bf16[16,6,2,16,1024]{4,3,2,1,0:T(8,128)(2,1)} %dynamic-slice_bitcast_fusion.2, f32[6]{0:T(128)S(1)} %get-tuple-element.323, bf16[2,16,6,2,16,1024]{5,4,3,2,1,0:T(8,128)(2,1)} %get-tuple-element.318, s32[]{:T(128)S(6)} %select_n.101, f32[]{:T(128)} %bitcast.41, f32[]{:T(128)} %bitcast.42, ...), kind=kLoop, calls=%fused_computation.10.clone.1 | loop fusion | flops 94339072 | bytes 12714048 | tf_op jit(solution)/shard_map/while/body/eval_jaxpr/reduce_sum | solution.py:72
  476.3 0.6 dynamic_slice.85
  477.6 6.8 %dynamic-slice_bitcast_fusion.2 = bf16[16,6,2,16,1024]{4,3,2,1,0:T(8,128)(2,1)} fusion(bf16[2,16,6,2,16,1024]{5,4,3,2,1,0:T(8,128)(2,1)} %get-tuple-element.317, s32[]{:T(128)S(6)} %select_n.99), kind=kLoop, calls=%fused_computation.11.clone.1 | loop fusion | bytes 12582916 | tf_op jit(solution)/shard_map/while/body/eval_jaxpr/jit(dynamic_index_in_dim)/squeeze | solution.py:106
  484.4 0.7 constant_dynamic-slice_fusion.6
  485.0 0.7 fusion.32
  485.7 31.1 %fusion.33 = f32[2,16,1024]{2,1,0:T(8,128)S(1)} fusion(bf16[16,6,2,16,1024]{4,3,2,1,0:T(8,128)(2,1)} %dynamic-slice_bitcast_fusion.2, f32[6]{0:T(128)S(1)} %get-tuple-element.323, bf16[2,16,6,2,16,1024]{5,4,3,2,1,0:T(8,128)(2,1)} %get-tuple-element.318, s32[]{:T(128)S(6)} %select_n.101, f32[]{:T(128)} %bitcast.41, f32[]{:T(128)} %bitcast.42, ...), kind=kLoop, calls=%fused_computation.10.clone.1 | loop fusion | flops 94339072 | bytes 12714048 | tf_op jit(solution)/shard_map/while/body/eval_jaxpr/reduce_sum | solution.py:72
  516.8 0.6 dynamic_slice.85
  518.1 0.7 copy-done.3
  518.7 0.0 all-reduce.6.cloned.1.call-update
  518.8 0.6 dynamic-slice
  520.0 33.4 %all-reduce.6.cloned.1.call-done = f32[2,2,16,1024]{3,2,1,0:T(8,128)} async-done(((f32[2,2,16,1024]{3,2,1,0:T(8,128)}), f32[2,2,16,1024]{3,2,1,0:T(8,128)}) %all-reduce.6.cloned.1.call-update) | async-done | bytes 262160
  553.4 1.5 constant_dynamic-slice_fusion.4
  (24 shorter events, 0.2 us)
Async XLA Ops:
  6.5 546.9 %all-reduce.6.cloned.1.call-start = ((), (), s32[]{:S(2)}) async-start(), calls=%async_computation | async-start | bytes 524288
  8.1 72.2 %collective-permute-start = (bf16[8,3,2,16,1024]{4,3,2,1,0:T(8,128)(2,1)S(1)}, bf16[8,3,2,16,1024]{4,3,2,1,0:T(8,128)(2,1)S(1)}, u32[]{:S(2)}, u32[]{:S(2)}) collective-permute-start(bf16[8,3,2,16,1024]{4,3,2,1,0:T(8,128)(2,1)S(1)} %constant_dynamic-slice_fusion.3), channel_id=1, source_target_pairs={{0,1},{1,2},{2,3},{3,4},{4,5},{5,6},{6,7},{8,9},{9,10},{10,11},{11... | collective-permute-start | bytes 4718600 | tf_op jit(solution)/shard_map/ppermute | solution.py:14
  13.1 67.2 %collective-permute-start.1 = (bf16[8,3,2,16,1024]{4,3,2,1,0:T(8,128)(2,1)S(1)}, bf16[8,3,2,16,1024]{4,3,2,1,0:T(8,128)(2,1)S(1)}, u32[]{:S(2)}, u32[]{:S(2)}) collective-permute-start(bf16[8,3,2,16,1024]{4,3,2,1,0:T(8,128)(2,1)S(1)} %constant_dynamic-slice_fusion.3), channel_id=1, source_target_pairs={{1,0},{2,1},{3,2},{4,3},{5,4},{6,5},{7,6},{9,8},{10,9},{11,10},{12... | collective-permute-start | bytes 4718600 | tf_op jit(solution)/shard_map/ppermute | solution.py:15
  80.6 36.7 %collective-permute-start.2 = (bf16[8,3,4,16,1024]{4,3,2,1,0:T(8,128)(2,1)S(1)}, bf16[8,3,4,16,1024]{4,3,2,1,0:T(8,128)(2,1)S(1)}, u32[]{:S(2)}, u32[]{:S(2)}) collective-permute-start(bf16[8,3,4,16,1024]{4,3,2,1,0:T(8,128)(2,1)S(1)} %pad_maximum_fusion), channel_id=1, source_target_pairs={{0,8},{8,16},{16,24},{24,0},{1,9},{9,17},{17,25},{25,1},{2,10},{10... | collective-permute-start | bytes 9437192 | tf_op jit(solution)/shard_map/ppermute | solution.py:86
  117.4 1.6 copy-start.1
  119.0 36.8 %collective-permute-start.3 = (bf16[8,3,4,16,1024]{4,3,2,1,0:T(8,128)(2,1)S(1)}, bf16[8,3,4,16,1024]{4,3,2,1,0:T(8,128)(2,1)}, u32[]{:S(2)}, u32[]{:S(2)}) collective-permute-start(bf16[8,3,4,16,1024]{4,3,2,1,0:T(8,128)(2,1)S(1)} %collective-permute-done.2), channel_id=1, source_target_pairs={{0,8},{8,16},{16,24},{24,0},{1,9},{9,17},{17,25},{25,1},{2,10},{10... | collective-permute-start | bytes 9437192 | tf_op jit(solution)/shard_map/ppermute | solution.py:86
  155.8 37.0 %collective-permute-start.4 = (bf16[8,3,4,16,1024]{4,3,2,1,0:T(8,128)(2,1)}, bf16[8,3,4,16,1024]{4,3,2,1,0:T(8,128)(2,1)}, u32[]{:S(2)}, u32[]{:S(2)}) collective-permute-start(bf16[8,3,4,16,1024]{4,3,2,1,0:T(8,128)(2,1)} %collective-permute-done.3), channel_id=1, source_target_pairs={{0,8},{8,16},{16,24},{24,0},{1,9},{9,17},{17,25},{25,1},{2,10},{10... | collective-permute-start | bytes 9437192 | tf_op jit(solution)/shard_map/ppermute | solution.py:86
  156.6 44.5 %copy-start.2 = (bf16[8,3,4,16,1024]{4,3,2,1,0:T(8,128)(2,1)S(1)}, bf16[8,3,4,16,1024]{4,3,2,1,0:T(8,128)(2,1)}, u32[]{:S(2)}) copy-start(bf16[8,3,4,16,1024]{4,3,2,1,0:T(8,128)(2,1)} %copy-done.1) | copy-start | bytes 9437188
  283.4 43.4 %copy-start.5 = (f32[2,16,1024]{2,1,0:T(8,128)S(1)}, f32[2,16,1024]{2,1,0:T(8,128)}, u32[]{:S(2)}) copy-start(f32[2,16,1024]{2,1,0:T(8,128)} %param.11) | copy-start | bytes 393220
  333.2 7.0 %copy-start.4 = (f32[2,16,1024]{2,1,0:T(8,128)S(1)}, f32[2,16,1024]{2,1,0:T(8,128)}, u32[]{:S(2)}) copy-start(f32[2,16,1024]{2,1,0:T(8,128)} %param.12) | copy-start | bytes 393220
  333.2 11.7 %slice-start = ((s8[12582912]{0:T(1024)(128)(4,1)}), s8[4194304]{0:T(1024)(128)(4,1)S(1)}, s32[]{:S(2)}) async-start(s8[12582912]{0:T(1024)(128)(4,1)} %bitcast.51), calls=%async_computation.1 | async-start | bytes 8388608
  336.7 8.3 %slice-start.1 = ((s8[12582912]{0:T(1024)(128)(4,1)}), s8[4194304]{0:T(1024)(128)(4,1)S(1)}, s32[]{:S(2)}) async-start(s8[12582912]{0:T(1024)(128)(4,1)} %bitcast.51), calls=%async_computation.2 | async-start | bytes 8388608
  340.2 4.8 slice-start.2
  344.9 11.2 %copy-start.6 = (f32[6]{0:T(128)S(1)}, f32[6]{0:T(128)}, u32[]{:S(2)}) copy-start(f32[6]{0:T(128)} %constant.153.clone..sunk.2) | copy-start | bytes 76
  351.6 4.5 copy-start
  356.1 162.7 %copy-start.7 = (u32[32]{0:T(128)S(1)}, u32[32]{0:T(128)}, u32[]{:S(2)}) copy-start(u32[32]{0:T(128)} %constant.168) | copy-start | bytes 388
  518.0 0.7 copy-start.3
Sparse Core Ops, SparseCore 0:
  518.9 34.4 all-reduce.5
